TPU v7x, 256 devices: a whole 4x4x8 slice. The times are simulated.
256 devices in a mesh: segment: 2 (over x_lo), seq: 16 (over y, x_hi, core), mp: 8 (over z).
Axes of the slice: x: 4 (x_hi: 2, x_lo: 2; x = x_hi * 2 + x_lo), y: 4, z: 8, core: 2. Of those that a mesh axis runs over, the one named last changes fastest.
Arguments:
- enc_states: bfloat16 [4096, 4096], P('seq', 'mp'), may hold values from -6 to 6
- dec_states: bfloat16 [4096, 4096], P('seq', 'mp'), may hold values from -21 to 21
- section_weights: bfloat16 [2, 4096, 2, 4096], P('segment', None, None, 'mp'), may hold values from -3 to 3
- group_lengths: int32 [32], P('seq'), may hold values from 1 to 128, 3072 in all
Outputs:
- mixed: bfloat16 [4096, 4096], P('seq', ('segment', 'mp'))
Inputs may be any that keep to these rules, and one draw needn't show every extreme that they name: Rows c * 128 to c * 128 + group_lengths[c] - 1 of the memory are real, the rest of block c is padding.
All inputs are finite; a program needn't handle non-finite values.
Results may differ from a plain program's by a relative error of at most 0.018.
Values may be sent and summed in bfloat16 or wider, within the bound.
A program may use at most 128 MiB of HBM per device.

v0:
```python
import math
import jax
import jax.numpy as jnp
from jax import lax
from jax.sharding import PartitionSpec as P

DH = 256
GROUP = 128


def from_behind(value, axis, steps):
    count = lax.axis_size(axis)
    leading, last = (max(0, -steps), min(count, count - steps))
    return lax.ppermute(value, axis, [(source, source + steps) for source in range(leading, last)])


def local(enc_states, dec_states, section_weights, group_lengths):
    encoder_side = lax.axis_index("segment") == 0
    local_weight = section_weights[0]
    width = local_weight.shape[0]
    columns = local_weight.shape[2]
    enc_rows = enc_states.shape[0]
    dec_rows = dec_states.shape[0]
    heads = columns // DH
    scale = DH ** (-0.5)
    start_sums = (
        jnp.zeros((enc_rows, 2 * columns), jnp.float32),
        jnp.zeros((dec_rows, columns), jnp.float32),
    )
    pieces = (
        lax.all_gather(enc_states, "mp", axis=1, tiled=True),
        lax.all_gather(dec_states, "mp", axis=1, tiled=True),
    )
    rows_in = pieces[0].shape[1]

    def encoder_work(state):
        update = jnp.dot(
            pieces[0],
            local_weight.reshape(rows_in, 2 * columns),
            preferred_element_type=jnp.float32,
        )
        return (update, state[1])

    def decoder_work(state):
        update = jnp.dot(pieces[1], local_weight[:, 0, :], preferred_element_type=jnp.float32)
        return (state[0], update)

    memory_sum, query_sum = lax.cond(encoder_side, encoder_work, decoder_work, start_sums)
    memory = memory_sum.astype(jnp.bfloat16)
    queries = query_sum.astype(jnp.bfloat16).reshape(dec_rows, heads, DH)
    received = from_behind(memory, "segment", 1)
    start_state = (
        jnp.full((dec_rows, heads), -1e30, jnp.float32),
        jnp.zeros((dec_rows, heads), jnp.float32),
        jnp.zeros((dec_rows, heads, DH), jnp.float32),
    )
    carry = start_state
    memory_piece = lax.all_gather(received, "seq", axis=0, tiled=True)
    length_piece = lax.all_gather(group_lengths, "seq", axis=0, tiled=True)
    amount = memory_piece.shape[0]
    span = math.gcd(amount, 1024)
    block_total = amount // span
    memory_blocks = memory_piece.reshape(block_total, span, 2 * columns)
    length_blocks = length_piece.reshape(block_total, span // GROUP)

    def one_block(state, item):
        best, total, accum = state
        block, lengths = item
        block_keys = block[:, :columns].reshape(span, heads, DH)
        block_values = block[:, columns:].reshape(span, heads, DH)
        scores = (
            jnp.einsum("qhd,khd->qhk", queries, block_keys, preferred_element_type=jnp.float32)
            * scale
        )
        valid = (jnp.arange(GROUP)[None, :] < lengths[:, None]).reshape(span)
        scores = jnp.where(valid[None, None, :], scores, -1e30)
        new_best = jnp.maximum(best, jnp.max(scores, axis=2))
        shrink = jnp.exp(best - new_best)
        weights = jnp.exp(scores - new_best[:, :, None]).astype(jnp.bfloat16)
        total = total * shrink + jnp.sum(weights, axis=2, dtype=jnp.float32)
        accum = accum * shrink[:, :, None] + jnp.einsum(
            "qhk,khd->qhd", weights, block_values, preferred_element_type=jnp.float32
        )
        return ((new_best, total, accum), None)

    carry, _ = lax.scan(one_block, carry, (memory_blocks, length_blocks))
    best, total, accum = carry
    attended = (accum / total[:, :, None]).astype(jnp.bfloat16).reshape(dec_rows, columns)

    def no_term(operand):
        return jnp.zeros((dec_rows, width), jnp.float32)

    def output_term(operand):
        projected = lax.dot_general(
            operand,
            local_weight[:, 1, :],
            (((1,), (1,)), ((), ())),
            preferred_element_type=jnp.float32,
        )
        offset = lax.axis_index("mp") * columns
        current = lax.dynamic_slice_in_dim(projected, offset, columns, 1)
        return lax.dynamic_update_slice_in_dim(
            projected, current + dec_states.astype(jnp.float32), offset, 1
        )

    term = lax.cond(encoder_side, no_term, output_term, attended)
    return lax.psum_scatter(
        term.astype(jnp.bfloat16), ("segment", "mp"), scatter_dimension=1, tiled=True
    )


def solution(mesh):
    in_specs = (P("seq", "mp"), P("seq", "mp"), P("segment", None, None, "mp"), P("seq"))
    out_specs = P("seq", ("segment", "mp"))
    return jax.shard_map(local, mesh=mesh, in_specs=in_specs, out_specs=out_specs, check_vma=False)
```

profile of v0, /device:TPU:8, one launch (start us, length us, event | category | flops | bytes accessed | tf_op | source)
XLA Modules:
  0.0 328.2 jit_solution(9274638926449847188)
XLA Ops:
  6.5 0.7 all-gather.6.cloned.1.call-update
  7.3 0.0 all-gather.4.cloned.1.call-start
  7.3 0.7 all-gather.4.cloned.1.call-update
  8.0 0.0 all-gather.8.cloned.1.call-start
  8.1 8.0 %copy.20 = bf16[1,4096,2,512]{3,1,2,0:T(8,128)(2,1)} copy(bf16[1,4096,2,512]{3,2,1,0:T(2,128)(2,1)} %param.12) | data formatting | bytes 16777216 | tf_op args[2]
  16.0 37.2 %all-gather.6.cloned.1.call-done = bf16[256,4096]{1,0:T(8,128)(2,1)} async-done(((bf16[256,512]{1,0:T(8,128)(2,1)}), bf16[256,4096]{1,0:T(8,128)(2,1)}) %all-gather.6.cloned.1.call-update) | async-done | bytes 2097168 | tf_op jit(solution)/shard_map/all_gather | solution.py:31
  53.2 41.5 %all-gather.4.cloned.1.call-done = bf16[256,4096]{1,0:T(8,128)(2,1)} async-done(((bf16[256,512]{1,0:T(8,128)(2,1)}), bf16[256,4096]{1,0:T(8,128)(2,1)}) %all-gather.4.cloned.1.call-update) | async-done | bytes 2097168 | tf_op jit(solution)/shard_map/all_gather | solution.py:32
  94.7 15.2 %conditional.2 = (bf16[256,1024]{1,0:T(8,128)(2,1)S(1)}, bf16[256,512]{1,0:T(8,128)(2,1)S(1)}) conditional(s32[]{:T(128)} %convert_element_type.25, (bf16[4096,2,512]{2,0,1:T(8,128)(2,1)}, bf16[256,4096]{1,0:T(8,128)(2,1)}) %tuple.67, (bf16[1,4096,2,512]{3,2,1,0:T(2,128)(2,1)}, bf16[256,4096]{1,0:T(8,128)(2,1)}) %tuple.24), branch_computations={%region_0.0_spmd, %region_1.0_spmd} | conditional | flops 2147483648 | bytes 36438064 | solution.py:48
  94.7 9.5 %copy.18 = bf16[512,8,2,512]{3,1,2,0:T(8,128)(2,1)} copy(bf16[512,8,2,512]{3,2,1,0:T(2,128)(2,1)} %bitcast.70) | data formatting | bytes 16777216 | tf_op jit(solution)/shard_map/cond
  104.2 5.7 %fusion.14 = bf16[256,1024]{1,0:T(8,128)(2,1)S(1)} fusion(bf16[256,4096]{1,0:T(8,128)(2,1)S(1)} %copy-done.4, bf16[4096,1024]{1,0:T(8,128)(2,1)} %bitcast.75), kind=kOutput, calls=%fused_computation.28 | convolution fusion | flops 2147483648 | bytes 11010048 | tf_op jit(solution)/shard_map/cond/branch_1_fun/dot_general | solution.py:37
  109.9 1.3 collective-permute-start
  111.2 7.7 %collective-permute-done = bf16[256,1024]{1,0:T(8,128)(2,1)S(1)} collective-permute-done((bf16[256,1024]{1,0:T(8,128)(2,1)S(1)}, bf16[256,1024]{1,0:T(8,128)(2,1)S(1)}, u32[]{:S(2)}, u32[]{:S(2)}) %collective-permute-start) | collective-permute-done | bytes 524320 | tf_op jit(solution)/shard_map/ppermute | solution.py:14
  119.0 0.8 copy-done.3
  119.8 0.0 all-gather.8.cloned.1.call-update
  119.8 0.0 reduce-scatter.2.cloned.1.call-start
  119.9 0.6 dynamic-slice
  121.2 0.2 dynamic-update-slice
  121.4 12.5 %all-reduce = s32[32]{0:T(128)S(1)} all-reduce(s32[32]{0:T(128)S(1)} %dynamic-update-slice), channel_id=1, replica_groups=mesh['segment'=2,'seq'=16,'mp'=8] {'seq'}, use_global_device_ids=true, to_apply=%add | all-reduce | flops 32 | bytes 256
  134.0 0.1 reshape.39
  134.0 0.1 copy.10
  134.2 0.1 copy.12
  134.3 61.9 %all-gather.8.cloned.1.call-done = bf16[4096,1024]{1,0:T(8,128)(2,1)} async-done(((bf16[256,1024]{1,0:T(8,128)(2,1)}), bf16[4096,1024]{1,0:T(8,128)(2,1)}) %all-gather.8.cloned.1.call-update) | async-done | bytes 8388624 | tf_op jit(solution)/shard_map/all_gather | solution.py:58
  196.2 39.4 %while.15 = (s32[]{:T(128)}, f32[256,2]{0,1:T(2,128)S(1)}, f32[256,2]{0,1:T(2,128)S(1)}, f32[256,2,256]{0,2,1:T(8,128)}, s32[4,8]{1,0:T(4,128)S(1)}, /*index=5*/...) while((s32[]{:T(128)}, f32[256,2]{0,1:T(2,128)S(1)}, ...), condition=%wide.region_5.6_spmd.clone, body=%wide.region_2.5_spmd.clone.sunk | while | flops 544083456 | bytes 26513672 | solution.py:86
  196.2 0.1 fusion.35
  196.3 3.1 constant_dynamic-slice_fusion.2
  199.4 2.9 copy.22
  202.3 0.2 fusion.36
  202.5 1.0 bitcast_reduce_fusion.2
  203.5 0.5 convert_reduce_fusion.2
  204.0 0.5 copy-done.1
  204.5 0.7 fusion.39
  205.3 0.8 copy-done.2
  206.1 0.1 fusion.35
  206.2 3.1 constant_dynamic-slice_fusion.2
  209.3 2.9 copy.22
  212.1 0.2 fusion.36
  212.3 1.0 bitcast_reduce_fusion.2
  213.4 0.5 convert_reduce_fusion.2
  213.9 0.5 copy-done.1
  214.4 0.7 fusion.39
  215.1 0.8 copy-done.2
  216.0 0.1 fusion.35
  216.0 3.1 constant_dynamic-slice_fusion.2
  219.1 2.9 copy.22
  222.0 0.2 fusion.36
  222.2 1.0 bitcast_reduce_fusion.2
  223.2 0.5 convert_reduce_fusion.2
  223.7 0.5 copy-done.1
  224.2 0.7 fusion.39
  225.0 0.8 copy-done.2
  225.8 0.1 fusion.35
  225.9 3.1 constant_dynamic-slice_fusion.2
  229.0 2.9 copy.22
  231.8 0.2 fusion.36
  232.0 1.0 bitcast_reduce_fusion.2
  233.1 0.5 convert_reduce_fusion.2
  233.6 0.5 copy-done.1
  234.1 0.7 fusion.39
  234.8 0.8 copy-done.2
  235.7 1.1 divide_convert_fusion
  236.7 2.5 conditional.3
  236.8 2.5 broadcast.17
  239.2 3.8 %convert_element_type.29 = bf16[256,4096]{1,0:T(8,128)(2,1)} convert(f32[256,4096]{1,0:T(8,128)} %get-tuple-element.217) | non-fusion elementwise | flops 1048576 | bytes 6291456 | tf_op jit(solution)/shard_map/convert_element_type | solution.py:108
  243.1 78.6 %reduce-scatter.2.cloned.1.call-done = bf16[256,256]{1,0:T(8,128)(2,1)} async-done(((bf16[256,4096]{1,0:T(8,128)(2,1)}), bf16[256,256]{1,0:T(8,128)(2,1)}) %reduce-scatter.2.cloned.1.call-update) | async-done | bytes 131088 | tf_op jit(solution)/shard_map/reduce_scatter | solution.py:107
  (38 shorter events, 0.2 us)
Async XLA Ops:
  6.5 46.6 %all-gather.6.cloned.1.call-start = ((), (), s32[]{:S(2)}) async-start(), calls=%async_computation.2 | async-start | bytes 2359296 | tf_op jit(solution)/shard_map/all_gather | solution.py:31
  7.3 87.4 %all-gather.4.cloned.1.call-start = ((), (), s32[]{:S(2)}) async-start(), calls=%async_computation.1 | async-start | bytes 2359296 | tf_op jit(solution)/shard_map/all_gather | solution.py:32
  8.0 188.2 %all-gather.8.cloned.1.call-start = ((), (), s32[]{:S(2)}) async-start(), calls=%async_computation.3 | async-start | bytes 8912896 | tf_op jit(solution)/shard_map/all_gather | solution.py:58
  94.7 25.2 %copy-start.6 = (u32[256]{0:T(256)S(1)}, u32[256]{0:T(256)}, u32[]{:S(2)}) copy-start(u32[256]{0:T(256)} %constant.50) | copy-start | bytes 3076
  94.7 26.5 %copy-start.5 = (s32[2]{0:T(128)S(1)}, s32[2]{0:T(128)}, u32[]{:S(2)}) copy-start(s32[2]{0:T(128)} %param.13) | copy-start | bytes 28
  94.7 9.5 %copy-start.4 = (bf16[256,4096]{1,0:T(8,128)(2,1)S(1)}, bf16[256,4096]{1,0:T(8,128)(2,1)}, u32[]{:S(2)}) copy-start(bf16[256,4096]{1,0:T(8,128)(2,1)} %get-tuple-element.53) | copy-start | bytes 6291460 | tf_op jit(solution)/shard_map/cond
  109.9 9.1 %collective-permute-start = (bf16[256,1024]{1,0:T(8,128)(2,1)S(1)}, bf16[256,1024]{1,0:T(8,128)(2,1)S(1)}, u32[]{:S(2)}, u32[]{:S(2)}) collective-permute-start(bf16[256,1024]{1,0:T(8,128)(2,1)S(1)} %get-tuple-element.70), channel_id=1, source_target_pairs={{0,128},{1,129},{2,130},{3,131},{4,132},{5,133},{6,134},{7,135},{8... | collective-permute-start | bytes 1572872 | tf_op jit(solution)/shard_map/ppermute | solution.py:14
  119.0 0.8 copy-start.3
  119.8 201.9 %reduce-scatter.2.cloned.1.call-start = ((), (), s32[]{:S(2)}) async-start(), calls=%async_computation.4 | async-start | bytes 2228224 | tf_op jit(solution)/shard_map/reduce_scatter | solution.py:107
  203.5 1.0 copy-start.1
  205.3 0.8 copy-start.2
  213.3 1.0 copy-start.1
  215.1 0.8 copy-start.2
  223.2 1.0 copy-start.1
  225.0 0.8 copy-start.2
  233.0 1.0 copy-start.1
  234.8 0.8 copy-start.2
Sparse Core Ops, SparseCore 0:
  9.1 43.9 all-gather.5
  55.0 39.6 all-gather.3
  119.9 76.2 all-gather.7
  243.2 78.4 reduce-scatter.1
where the time goes:
time: 329 us; the launch traced here: 328 us
  waiting for transfers between devices  228 us (69%)
  local copies, waits for them, and re-layouts  51.7 us (16%)
  between operations  13.9 us (4%)
  matrix products  12.7 us (4%)
  blocking collectives  12.5 us (4%)
  other arithmetic  7.33 us (2%)
    reduce_scatter x1, waiting for transfers between devices, local(): lax.psum_scatter(term.astype(jnp.bfloat16), ('segment', 'mp'), scatter_di...  78.6 us
    all_gather x1, waiting for transfers between devices, local(): memory_piece = lax.all_gather(received, 'seq', axis=0, tiled=True)  61.9 us
    all_gather x1, waiting for transfers between devices, local(): lax.all_gather(dec_states, 'mp', axis=1, tiled=True)  41.5 us
    all_gather x1, waiting for transfers between devices, local(): lax.all_gather(enc_states, 'mp', axis=1, tiled=True)  37.2 us
    dynamic_slice x8, local copies, waits for them, and re-layouts, local(): carry, _ = lax.scan(one_block, carry, (memory_blocks, length_blocks))  23.8 us
    unnamed x1, blocking collectives  12.5 us
    unnamed x11, local copies, waits for them, and re-layouts  9.78 us
    cond x3, local copies, waits for them, and re-layouts  9.49 us
  transfers between devices with their start and end apart: 5, of which 5 were waited for; matrix products, arithmetic and copies ran while one was open for 3% of the time, Pallas kernels for 0%

commit v1 on v0

--- a/solution.py
+++ b/solution.py
@@ -55,7 +55,9 @@
         jnp.zeros((dec_rows, heads, DH), jnp.float32),
     )
     carry = start_state
-    memory_piece = lax.all_gather(received, "seq", axis=0, tiled=True)
+    memory_piece = jnp.concatenate(
+        lax.all_to_all(jnp.stack([received] * lax.axis_size("seq")), "seq", 0, 0), axis=0
+    )
     length_piece = lax.all_gather(group_lengths, "seq", axis=0, tiled=True)
     amount = memory_piece.shape[0]
     span = math.gcd(amount, 1024)

time: 329 us -> 362 us (1.10)
  blocking collectives: 12.5 us -> 99.5 us
  waiting for transfers between devices: 228 us -> 164 us
  starting transfers between devices: 1.44 us -> 8.79 us
    unnamed x1, blocking collectives: 12.5 us -> 99.5 us
    all_gather x1 -> x0, waiting for transfers between devices: 61.9 us -> none  [local(): memory_piece = lax.all_gather(received, 'seq', axis=0, tiled=True)]
    all_to_all x0 -> x1, starting transfers between devices: none -> 7.39 us  [local(): lax.all_to_all(jnp.stack([received] * lax.axis_size('seq')), 'seq', 0, 0)]
    another operation x1 -> x2, local copies, waits for them, and re-layouts: 2.46 us -> 6.77 us  [the longest x1 4.32 us: local(): jnp.stack([received] * lax.axis_size('seq'))]
    unnamed x11 -> x9, local copies, waits for them, and re-layouts: 9.78 us -> 8.91 us
  transfers between devices with their start and end apart: 5 -> 5, of which waited for: 5 -> 4; matrix products, arithmetic and copies ran while one was open for 3% -> 3% of each run, Pallas kernels for 0% -> 0%
where the time goes in v1:
time: 362 us; the launch traced here: 361 us
  waiting for transfers between devices  164 us (45%)
  blocking collectives  99.5 us (27%)
  local copies, waits for them, and re-layouts  55.2 us (15%)
  between operations  13.8 us (4%)
  matrix products  12.7 us (4%)
  starting transfers between devices  8.79 us (2%)
  other arithmetic  7.31 us (2%)
    unnamed x1, blocking collectives  99.5 us
    reduce_scatter x1, waiting for transfers between devices, local(): lax.psum_scatter(term.astype(jnp.bfloat16), ('segment', 'mp'), scatter_di...  76 us
    all_gather x1, waiting for transfers between devices, local(): lax.all_gather(dec_states, 'mp', axis=1, tiled=True)  41.5 us
    all_gather x1, waiting for transfers between devices, local(): lax.all_gather(enc_states, 'mp', axis=1, tiled=True)  37.2 us
    dynamic_slice x8, local copies, waits for them, and re-layouts, local(): carry, _ = lax.scan(one_block, carry, (memory_blocks, length_blocks))  23.8 us
    cond x3, local copies, waits for them, and re-layouts  9.48 us
    unnamed x9, local copies, waits for them, and re-layouts  8.91 us
    ppermute x1, waiting for transfers between devices, from_behind(): lax.ppermute(value, axis, [(source, source + steps) for source in range(l...  7.72 us
  transfers between devices with their start and end apart: 5, of which 4 were waited for; matrix products, arithmetic and copies ran while one was open for 3% of the time, Pallas kernels for 0%

profile of v1, /device:TPU:8, one launch (start us, length us, event | category | flops | bytes accessed | tf_op | source)
XLA Modules:
  0.0 361.4 jit_solution(13337056072990007314)
XLA Ops:
  6.5 0.7 all-gather.5.cloned.1.call-update
  7.3 0.0 all-gather.3.cloned.1.call-start
  7.3 0.7 all-gather.3.cloned.1.call-update
  8.0 7.9 %copy.20 = bf16[1,4096,2,512]{3,1,2,0:T(8,128)(2,1)} copy(bf16[1,4096,2,512]{3,2,1,0:T(2,128)(2,1)} %param.12) | data formatting | bytes 16777216 | tf_op args[2]
  16.0 37.2 %all-gather.5.cloned.1.call-done = bf16[256,4096]{1,0:T(8,128)(2,1)} async-done(((bf16[256,512]{1,0:T(8,128)(2,1)}), bf16[256,4096]{1,0:T(8,128)(2,1)}) %all-gather.5.cloned.1.call-update) | async-done | bytes 2097168 | tf_op jit(solution)/shard_map/all_gather | solution.py:31
  53.2 41.5 %all-gather.3.cloned.1.call-done = bf16[256,4096]{1,0:T(8,128)(2,1)} async-done(((bf16[256,512]{1,0:T(8,128)(2,1)}), bf16[256,4096]{1,0:T(8,128)(2,1)}) %all-gather.3.cloned.1.call-update) | async-done | bytes 2097168 | tf_op jit(solution)/shard_map/all_gather | solution.py:32
  94.7 15.2 %conditional.2 = (bf16[256,1024]{1,0:T(8,128)(2,1)S(1)}, bf16[256,512]{1,0:T(8,128)(2,1)S(1)}) conditional(s32[]{:T(128)} %convert_element_type.25, (bf16[4096,2,512]{2,0,1:T(8,128)(2,1)}, bf16[256,4096]{1,0:T(8,128)(2,1)}) %tuple.65, (bf16[1,4096,2,512]{3,2,1,0:T(2,128)(2,1)}, bf16[256,4096]{1,0:T(8,128)(2,1)}) %tuple.24), branch_computations={%region_0.0_spmd, %region_1.0_spmd} | conditional | flops 2147483648 | bytes 36438064 | solution.py:48
  94.7 9.5 %copy.18 = bf16[512,8,2,512]{3,1,2,0:T(8,128)(2,1)} copy(bf16[512,8,2,512]{3,2,1,0:T(2,128)(2,1)} %bitcast.70) | data formatting | bytes 16777216 | tf_op jit(solution)/shard_map/cond
  104.2 5.7 %fusion.14 = bf16[256,1024]{1,0:T(8,128)(2,1)S(1)} fusion(bf16[256,4096]{1,0:T(8,128)(2,1)S(1)} %copy-done.3, bf16[4096,1024]{1,0:T(8,128)(2,1)} %bitcast.74), kind=kOutput, calls=%fused_computation.28 | convolution fusion | flops 2147483648 | bytes 11010048 | tf_op jit(solution)/shard_map/cond/branch_1_fun/dot_general | solution.py:37
  109.9 1.3 collective-permute-start
  111.2 7.7 %collective-permute-done = bf16[256,1024]{1,0:T(8,128)(2,1)S(1)} collective-permute-done((bf16[256,1024]{1,0:T(8,128)(2,1)S(1)}, bf16[256,1024]{1,0:T(8,128)(2,1)S(1)}, u32[]{:S(2)}, u32[]{:S(2)}) %collective-permute-start) | collective-permute-done | bytes 524320 | tf_op jit(solution)/shard_map/ppermute | solution.py:14
  119.0 4.3 %stack.2 = bf16[16,256,1024]{2,1,0:T(8,128)(2,1)} broadcast(bf16[256,1024]{1,0:T(8,128)(2,1)S(1)} %collective-permute-done), dimensions={1,2} | broadcast | bytes 8912896 | tf_op jit(solution)/shard_map/stack | solution.py:59
  123.3 7.4 %all-to-all-start = ((bf16[16,256,1024]{2,1,0:T(8,128)(2,1)}), bf16[16,256,1024]{2,1,0:T(8,128)(2,1)}, u32[]{:S(2)}, u32[]{:S(2)}) async-start(bf16[16,256,1024]{2,1,0:T(8,128)(2,1)} %stack.2), calls=%async_computation | async-start | bytes 16777216 | tf_op jit(solution)/shard_map/all_to_all | solution.py:59
  130.7 0.0 reduce-scatter.2.cloned.1.call-start
  130.8 0.6 dynamic-slice
  131.9 0.2 dynamic-update-slice
  132.2 99.5 %all-reduce = s32[32]{0:T(128)S(1)} all-reduce(s32[32]{0:T(128)S(1)} %dynamic-update-slice), channel_id=1, replica_groups=mesh['segment'=2,'seq'=16,'mp'=8] {'seq'}, use_global_device_ids=true, to_apply=%add | all-reduce | flops 32 | bytes 256
  231.7 0.1 reshape.38
  231.8 0.1 copy.10
  231.9 0.1 copy.12
  232.1 0.0 all-to-all-done
  232.1 39.5 %while.15 = (s32[]{:T(128)}, f32[256,2]{0,1:T(2,128)S(1)}, f32[256,2]{0,1:T(2,128)S(1)}, f32[256,2,256]{0,2,1:T(8,128)}, s32[4,8]{1,0:T(4,128)S(1)}, /*index=5*/...) while((s32[]{:T(128)}, f32[256,2]{0,1:T(2,128)S(1)}, ...), condition=%wide.region_5.6_spmd.clone, body=%wide.region_2.5_spmd.clone.sunk | while | flops 544083456 | bytes 26513672 | solution.py:88
  232.1 0.1 fusion.35
  232.2 3.1 constant_dynamic-slice_fusion.2
  235.3 2.9 copy.22
  238.1 0.2 fusion.36
  238.3 1.0 bitcast_reduce_fusion.2
  239.4 0.5 convert_reduce_fusion.2
  239.9 0.5 copy-done.1
  240.4 0.7 fusion.39
  241.1 0.8 copy-done.2
  242.0 0.1 fusion.35
  242.1 3.1 constant_dynamic-slice_fusion.2
  245.1 2.9 copy.22
  248.0 0.2 fusion.36
  248.2 1.0 bitcast_reduce_fusion.2
  249.2 0.5 convert_reduce_fusion.2
  249.8 0.5 copy-done.1
  250.2 0.7 fusion.39
  251.0 0.8 copy-done.2
  251.8 0.1 fusion.35
  251.9 3.1 constant_dynamic-slice_fusion.2
  255.0 2.9 copy.22
  257.9 0.2 fusion.36
  258.1 1.0 bitcast_reduce_fusion.2
  259.1 0.5 convert_reduce_fusion.2
  259.6 0.5 copy-done.1
  260.1 0.7 fusion.39
  260.9 0.8 copy-done.2
  261.7 0.1 fusion.35
  261.8 3.1 constant_dynamic-slice_fusion.2
  264.9 2.9 copy.22
  267.7 0.2 fusion.36
  267.9 1.0 bitcast_reduce_fusion.2
  269.0 0.5 convert_reduce_fusion.2
  269.5 0.5 copy-done.1
  270.0 0.7 fusion.39
  270.7 0.8 copy-done.2
  271.6 1.1 divide_convert_fusion
  272.6 2.5 conditional.3
  272.7 2.5 broadcast.19
  275.1 3.8 %convert_element_type.29 = bf16[256,4096]{1,0:T(8,128)(2,1)} convert(f32[256,4096]{1,0:T(8,128)} %get-tuple-element.217) | non-fusion elementwise | flops 1048576 | bytes 6291456 | tf_op jit(solution)/shard_map/convert_element_type | solution.py:110
  278.9 0.0 reduce-scatter.2.cloned.1.call-update
  278.9 76.0 %reduce-scatter.2.cloned.1.call-done = bf16[256,256]{1,0:T(8,128)(2,1)} async-done(((bf16[256,4096]{1,0:T(8,128)(2,1)}), bf16[256,256]{1,0:T(8,128)(2,1)}) %reduce-scatter.2.cloned.1.call-update) | async-done | bytes 131088 | tf_op jit(solution)/shard_map/reduce_scatter | solution.py:109
  (36 shorter events, 0.2 us)
Async XLA Ops:
  6.5 46.6 %all-gather.5.cloned.1.call-start = ((), (), s32[]{:S(2)}) async-start(), calls=%async_computation.3 | async-start | bytes 2359296 | tf_op jit(solution)/shard_map/all_gather | solution.py:31
  7.3 87.4 %all-gather.3.cloned.1.call-start = ((), (), s32[]{:S(2)}) async-start(), calls=%async_computation.2 | async-start | bytes 2359296 | tf_op jit(solution)/shard_map/all_gather | solution.py:32
  94.7 9.5 %copy-start.3 = (bf16[256,4096]{1,0:T(8,128)(2,1)S(1)}, bf16[256,4096]{1,0:T(8,128)(2,1)}, u32[]{:S(2)}) copy-start(bf16[256,4096]{1,0:T(8,128)(2,1)} %get-tuple-element.53) | copy-start | bytes 6291460 | tf_op jit(solution)/shard_map/cond
  109.9 9.1 %collective-permute-start = (bf16[256,1024]{1,0:T(8,128)(2,1)S(1)}, bf16[256,1024]{1,0:T(8,128)(2,1)S(1)}, u32[]{:S(2)}, u32[]{:S(2)}) collective-permute-start(bf16[256,1024]{1,0:T(8,128)(2,1)S(1)} %get-tuple-element.70), channel_id=1, source_target_pairs={{0,128},{1,129},{2,130},{3,131},{4,132},{5,133},{6,134},{7,135},{8... | collective-permute-start | bytes 1572872 | tf_op jit(solution)/shard_map/ppermute | solution.py:14
  123.3 7.5 %copy-start.5 = (u32[256]{0:T(256)S(1)}, u32[256]{0:T(256)}, u32[]{:S(2)}) copy-start(u32[256]{0:T(256)} %constant.50) | copy-start | bytes 3076
  123.3 8.7 %copy-start.4 = (s32[2]{0:T(128)S(1)}, s32[2]{0:T(128)}, u32[]{:S(2)}) copy-start(s32[2]{0:T(128)} %param.13) | copy-start | bytes 28
  123.3 108.8 %all-to-all-start = ((bf16[16,256,1024]{2,1,0:T(8,128)(2,1)}), bf16[16,256,1024]{2,1,0:T(8,128)(2,1)}, u32[]{:S(2)}, u32[]{:S(2)}) async-start(bf16[16,256,1024]{2,1,0:T(8,128)(2,1)} %stack.2), calls=%async_computation | async-start | bytes 16777216 | tf_op jit(solution)/shard_map/all_to_all | solution.py:59
  130.7 224.2 %reduce-scatter.2.cloned.1.call-start = ((), (), s32[]{:S(2)}) async-start(), calls=%async_computation.4 | async-start | bytes 2228224 | tf_op jit(solution)/shard_map/reduce_scatter | solution.py:109
  239.3 1.0 copy-start.1
  241.1 0.8 copy-start.2
  249.2 1.0 copy-start.1
  251.0 0.8 copy-start.2
  259.1 1.0 copy-start.1
  260.9 0.8 copy-start.2
  268.9 1.0 copy-start.1
  270.7 0.8 copy-start.2
Sparse Core Ops, SparseCore 0:
  9.1 43.9 all-gather.4
  55.0 39.6 all-gather.2
  279.1 75.8 reduce-scatter.1
